TPU v7x, 512 devices: a whole 4x4x16 slice. The times are simulated.
512 devices in a mesh: ctx: 64 (over z, y), head: 8 (over x, core).
Axes of the slice: x: 4, y: 4, z: 16, core: 2. Of those that a mesh axis runs over, the one named last changes fastest.
Arguments:
- lin_queries: bfloat16 [16384, 8192], P('ctx', 'head'), may hold values from -6 to 6
- lin_keys: bfloat16 [16384, 8192], P('ctx', 'head'), may hold values from -6 to 6
- lin_values: bfloat16 [16384, 8192], P('ctx', 'head'), may hold values from -21 to 21
- log_decay: float32 [16384, 64], P('ctx', 'head'), may hold values from -1 to 0
- lin_gate: bfloat16 [16384, 8192], P('ctx', 'head'), may hold values from -6 to 6
- norm_gain: float32 [8192], P('head'), may hold values from 0.1 to 1.9
- soft_queries: bfloat16 [16384, 8192], P('ctx', 'head'), may hold values from -6 to 6
- slab_keys: bfloat16 [16384, 1024], P('ctx', 'head'), may hold values from -6 to 6
- slab_values: bfloat16 [16384, 1024], P('ctx', 'head'), may hold values from -6 to 6
- cache_keys: bfloat16 [65536, 1024], P('ctx', 'head'), may hold values from -6 to 6
- cache_values: bfloat16 [65536, 1024], P('ctx', 'head'), may hold values from -6 to 6
- block_lists: int32 [128, 16], replicated, may hold values from 0 to 511, as said below
- live_counts: int32 [128], replicated, may hold values from 2 to 16
Outputs:
- lin_out: bfloat16 [16384, 8192], P('ctx', 'head')
- soft_out: bfloat16 [16384, 8192], P('ctx', 'head')
Inputs may be any that keep to these rules, and one draw needn't show every extreme that they name: `block_lists`: cache block g lies on ctx index g // 8. One list names 16 blocks on 16 different ctx indices, and all lists of the 2 query blocks of one ctx index name at most one block of any one ctx index. Entries from live_counts on are not read.
All inputs are finite; a program needn't handle non-finite values.
Results may differ from a plain program's by a relative error of at most 0.0046.
Values may be sent and summed in bfloat16 or wider, within the bound.
A program may use at most 128 MiB of HBM per device.

v0:
```python
import math

import jax
import jax.numpy as jnp
from jax import lax
from jax.sharding import PartitionSpec as P

QUERY_HEADS = 64
HD = 128
BLOCK = 128


def entering_2(array, axis, combine, identity):
    count, index = (lax.axis_size(axis), lax.axis_index(axis))
    everything = jax.tree.map(lambda part: lax.all_gather(part, axis), array)
    start = jax.tree.map(
        lambda part, zero: jnp.broadcast_to(jnp.asarray(zero, part.dtype), part.shape),
        array,
        identity,
    )

    def turn(k, before):
        reached = k < index
        new = combine(before, jax.tree.map(lambda part: part[k], everything))
        return jax.tree.map(lambda a, b: jnp.where(reached, a, b), new, before)

    return lax.fori_loop(0, count, turn, start)


def combine_states(earlier, later):
    early_total, early_state = earlier
    late_total, late_state = later
    return (early_total + late_total, jnp.exp(late_total)[:, None, None] * early_state + late_state)


def lightning(lin_queries, lin_keys, lin_values, log_decay, lin_gate, norm_gain):
    tok_rows = lin_queries.shape[0]
    head_count = lin_queries.shape[1] // HD
    act_queries = (
        jax.nn.silu(lin_queries.astype(jnp.float32))
        .astype(jnp.bfloat16)
        .reshape(tok_rows, head_count, HD)
    )
    act_keys = (
        jax.nn.silu(lin_keys.astype(jnp.float32))
        .astype(jnp.bfloat16)
        .reshape(tok_rows, head_count, HD)
    )
    values_here = lin_values.reshape(tok_rows, head_count, HD)
    running = jnp.cumsum(log_decay, axis=0)
    seg_total = running[-1]
    flipped = running.T
    gaps = flipped[:, :, None] - flipped[:, None, :]
    causal = jnp.arange(tok_rows)[:, None] >= jnp.arange(tok_rows)[None, :]
    weight = jnp.where(causal[None], jnp.exp(jnp.minimum(gaps, 0.0)), 0.0)
    scores = jnp.einsum("thd,shd->hts", act_queries, act_keys, preferred_element_type=jnp.float32)
    lin_scores = (scores * weight).astype(jnp.bfloat16)
    intra = jnp.einsum("hts,shd->thd", lin_scores, values_here, preferred_element_type=jnp.float32)
    fade = jnp.exp(seg_total[None, :] - running)
    seg_state = jnp.einsum(
        "shd,she->hde",
        act_keys.astype(jnp.float32) * fade[:, :, None],
        values_here.astype(jnp.float32),
        precision=lax.Precision.HIGHEST,
    )
    empty_total = jnp.zeros((head_count,), jnp.float32)
    empty_state = jnp.zeros((head_count, HD, HD), jnp.float32)
    unused, entering = entering_2(
        (seg_total, seg_state), "ctx", combine_states, (empty_total, empty_state)
    )
    inter = jnp.exp(running)[:, :, None] * jnp.einsum(
        "thd,hde->the", act_queries.astype(jnp.float32), entering, precision=lax.Precision.HIGHEST
    )
    lin_attn = (intra + inter).reshape(tok_rows, head_count * HD)
    partial_squares = jnp.sum(lin_attn * lin_attn, axis=1)
    whole_squares = lax.psum(partial_squares, "head")
    scaling = lax.rsqrt(whole_squares / (QUERY_HEADS * HD) + 1e-06)
    gated = (
        lin_attn
        * scaling[:, None]
        * norm_gain[None, :]
        * jax.nn.sigmoid(lin_gate.astype(jnp.float32))
    )
    return gated.astype(jnp.bfloat16)


def cache_attention(
    soft_queries, slab_keys, slab_values, cache_keys, cache_values, block_lists, live_counts
):
    tok_rows = soft_queries.shape[0]
    blocks_here = tok_rows // BLOCK
    kv_count = cache_keys.shape[1] // HD
    group_size = soft_queries.shape[1] // HD // kv_count
    ctx_devices = lax.axis_size("ctx")
    my_place = lax.axis_index("ctx")
    stored = cache_keys.shape[0] // BLOCK
    selected = block_lists.shape[1]
    packed = jnp.concatenate(
        [
            cache_keys.reshape(stored, BLOCK, kv_count, HD),
            cache_values.reshape(stored, BLOCK, kv_count, HD),
        ],
        axis=3,
    )
    packed = packed.reshape(stored, BLOCK * kv_count * 2 * HD)
    owner_of = block_lists // stored
    spot_of = block_lists % stored
    matches = (spot_of[:, :, None] == jnp.arange(stored, dtype=jnp.int32)[None, None, :]) & (
        owner_of == my_place
    )[:, :, None]
    my_owners = lax.dynamic_slice_in_dim(owner_of, my_place * blocks_here, blocks_here, 0)
    my_counts = lax.dynamic_slice_in_dim(live_counts, my_place * blocks_here, blocks_here, 0)
    wanted = jnp.any(matches, axis=1)
    outgoing = jnp.dot(
        wanted.astype(jnp.bfloat16), packed, preferred_element_type=jnp.float32
    ).astype(jnp.bfloat16)
    outgoing = outgoing.reshape(ctx_devices, blocks_here, BLOCK, kv_count, 2 * HD)
    arrived = lax.all_to_all(outgoing, "ctx", split_axis=0, concat_axis=0, tiled=True)
    fetched = [arrived[my_owners[block_index], block_index] for block_index in range(blocks_here)]
    local_keys = slab_keys.reshape(tok_rows, kv_count, HD)
    local_values = slab_values.reshape(tok_rows, kv_count, HD)
    inverse_root = 1.0 / math.sqrt(HD)
    results = []
    for block_index in range(blocks_here):
        kv_rows = fetched[block_index].reshape(selected * BLOCK, kv_count, 2 * HD)
        all_keys = jnp.concatenate([kv_rows[:, :, :HD], local_keys], axis=0)
        all_values = jnp.concatenate([kv_rows[:, :, HD:], local_values], axis=0)
        queries = soft_queries[block_index * BLOCK : (block_index + 1) * BLOCK].reshape(
            BLOCK, kv_count, group_size, HD
        )
        scores = (
            jnp.einsum("tkgd,skd->kgts", queries, all_keys, preferred_element_type=jnp.float32)
            * inverse_root
        )
        cache_live = jnp.arange(selected * BLOCK) // BLOCK < my_counts[block_index]
        positions = block_index * BLOCK + jnp.arange(BLOCK)
        causal = jnp.arange(tok_rows)[None, :] <= positions[:, None]
        allowed = jnp.concatenate(
            [jnp.broadcast_to(cache_live[None, :], (BLOCK, selected * BLOCK)), causal], axis=1
        )
        scores = jnp.where(allowed[None, None], scores, -1e30)
        highest = jnp.max(scores, axis=3, keepdims=True)
        weights = jnp.exp(scores - highest)
        totals = jnp.sum(weights, axis=3)
        mixed = jnp.einsum(
            "kgts,skd->tkgd",
            weights.astype(jnp.bfloat16),
            all_values,
            preferred_element_type=jnp.float32,
        )
        normed = mixed / jnp.transpose(totals, (2, 0, 1))[:, :, :, None]
        results.append(normed.astype(jnp.bfloat16).reshape(BLOCK, kv_count * group_size * HD))
    return jnp.concatenate(results, axis=0)


def local(
    lin_queries,
    lin_keys,
    lin_values,
    log_decay,
    lin_gate,
    norm_gain,
    soft_queries,
    slab_keys,
    slab_values,
    cache_keys,
    cache_values,
    block_lists,
    live_counts,
):
    lin_out = lightning(lin_queries, lin_keys, lin_values, log_decay, lin_gate, norm_gain)
    soft_out = cache_attention(
        soft_queries, slab_keys, slab_values, cache_keys, cache_values, block_lists, live_counts
    )
    return (lin_out, soft_out)


def solution(mesh):
    in_specs = (
        P("ctx", "head"),
        P("ctx", "head"),
        P("ctx", "head"),
        P("ctx", "head"),
        P("ctx", "head"),
        P("head"),
        P("ctx", "head"),
        P("ctx", "head"),
        P("ctx", "head"),
        P("ctx", "head"),
        P("ctx", "head"),
        P(),
        P(),
    )
    out_specs = (P("ctx", "head"), P("ctx", "head"))
    return jax.shard_map(local, mesh=mesh, in_specs=in_specs, out_specs=out_specs, check_vma=False)
```

profile of v0, /device:TPU:16, one launch (start us, length us, event | category | flops | bytes accessed | tf_op | source)
XLA Modules:
  0.0 761.5 jit_solution(15208732093113824925)
XLA Ops:
  7.2 1.3 reduce-window.6
  9.0 1.4 fusion.32
  10.6 1.5 fusion.33
  15.0 5.6 convolution_convert_fusion
  20.6 9.1 %copy.126 = bf16[16,8,128,256]{3,2,1,0:T(8,128)(2,1)} copy(bf16[16,8,128,256]{3,1,2,0:T(8,128)(2,1)} %bitcast.204) | data formatting | bytes 16777216
  29.6 18.9 %all-to-all-start = ((bf16[64,2,128,1,256]{4,2,1,3,0:T(8,128)(2,1)}), bf16[64,2,128,1,256]{4,2,1,3,0:T(8,128)(2,1)}, u32[]{:S(2)}, u32[]{:S(2)}) async-start(bf16[64,2,128,1,256]{4,2,1,3,0:T(8,128)(2,1)} %bitcast.203), calls=%async_computation | async-start | bytes 16777216 | tf_op jit(solution)/shard_map/all_to_all | solution.py:118
  51.9 511.1 %all-gather.1 = f32[64,1,8]{2,1,0:T(1,128)} all-gather(f32[1,1,8]{2,1,0:T(1,128)S(1)} %bitcast.220), channel_id=1, replica_groups=mesh['ctx'=64,'head'=8] {'ctx'}, dimensions={0}, use_global_device_ids=true | all-gather | bytes 2080 | tf_op jit(solution)/shard_map/all_gather | solution.py:15
  563.7 2.2 pad_add_fusion.1
  565.9 2.4 pad_add_fusion
  568.3 4.1 gather_fusion.1
  572.5 2.3 fusion.6
  574.8 1.9 fusion.3
  576.8 2.3 fusion.49
  579.2 4.1 gather_fusion
  583.4 2.3 fusion.5
  585.7 1.9 fusion.1
  587.7 2.3 fusion.43
  591.0 21.6 %all-gather.4.cloned.1.call-done = f32[512,128,128]{2,1,0:T(8,128)} async-done(((f32[8,128,128]{2,1,0:T(8,128)}), f32[512,128,128]{2,1,0:T(8,128)}) %all-gather.4.cloned.1.call-update) | async-done | bytes 33554448 | tf_op jit(solution)/shard_map/all_gather | solution.py:15
  612.5 120.5 %while.14 = (s32[]{:T(128)}, f32[8,128,128]{2,1,0:T(8,128)S(1)}, s32[]{:T(128)}, f32[64,8]{1,0:T(8,128)}, f32[64,8,128,128]{3,2,1,0:T(8,128)}, /*index=5*/s32[]{:T(128)}, s32[]{:T(128)}) while((s32[]{:T(128)}, f32[8,128,128]{2,1,0:T(8,128)S(1)}, s32[]{:T(128)}, f32[64,8]{1,0:T(8,128)}, f32[64,8,128,128]{3,2,1,0:T(8,128)}, ...), condition=%wide.region_3.4_spmd.clone, body=%wide.region_2.3_spmd.clone.sunk | while | flops 524292 | bytes 1573073 | solution.py:27
  615.1 1.2 fusion.124
  617.0 1.2 fusion.124
  618.9 1.2 fusion.124
  620.8 1.2 fusion.124
  622.7 1.2 fusion.124
  624.5 1.2 fusion.124
  626.4 1.2 fusion.124
  628.3 1.2 fusion.124
  630.2 1.2 fusion.124
  632.1 1.2 fusion.124
  634.0 1.2 fusion.124
  635.9 1.2 fusion.124
  637.7 1.2 fusion.124
  639.6 1.2 fusion.124
  641.5 1.2 fusion.124
  643.4 1.2 fusion.124
  647.1 1.2 fusion.124
  649.0 1.2 fusion.124
  650.9 1.2 fusion.124
  652.8 1.2 fusion.124
  654.6 1.2 fusion.124
  656.5 1.2 fusion.124
  658.4 1.2 fusion.124
  660.3 1.2 fusion.124
  664.0 1.2 fusion.124
  733.1 1.8 fusion.18
  734.9 2.5 multiply_reduce_fusion
  737.8 14.7 %psum.7 = f32[256]{0:T(256)S(1)} all-reduce(f32[256]{0:T(256)S(1)} %get-tuple-element.139), channel_id=1, replica_groups=mesh['ctx'=64,'head'=8] {'head'}, use_global_device_ids=true, to_apply=%region_5.6 | all-reduce | flops 256 | bytes 2048 | tf_op jit(solution)/shard_map/psum | solution.py:76
  752.5 2.2 multiply_convert_fusion.1
  (160 shorter events, 99.0 us)
Async XLA Ops:
  7.2 3.5 copy-start
  7.2 605.4 %all-gather.4.cloned.1.call-start = ((), (), s32[]{:S(2)}) async-start(), calls=%async_computation.1 | async-start | bytes 34078720 | tf_op jit(solution)/shard_map/all_gather | solution.py:15
  29.6 19.0 %copy-start.1 = (bf16[256,1024]{1,0:T(8,128)(2,1)S(1)}, bf16[256,1024]{1,0:T(8,128)(2,1)}, u32[]{:S(2)}) copy-start(bf16[256,1024]{1,0:T(8,128)(2,1)} %param.21) | copy-start | bytes 1572868
  29.6 19.2 %copy-start.8 = (s32[128]{0:T(128)S(1)}, s32[128]{0:T(128)}, u32[]{:S(2)}) copy-start(s32[128]{0:T(128)} %param.27) | copy-start | bytes 1540
  29.6 538.6 %all-to-all-start = ((bf16[64,2,128,1,256]{4,2,1,3,0:T(8,128)(2,1)}), bf16[64,2,128,1,256]{4,2,1,3,0:T(8,128)(2,1)}, u32[]{:S(2)}, u32[]{:S(2)}) async-start(bf16[64,2,128,1,256]{4,2,1,3,0:T(8,128)(2,1)} %bitcast.203), calls=%async_computation | async-start | bytes 16777216 | tf_op jit(solution)/shard_map/all_to_all | solution.py:118
  572.5 4.3 copy-start.6
  576.8 6.6 copy-start.2
  583.4 4.3 copy-start.7
  587.7 145.4 %copy-start.5 = (bf16[256,1024]{1,0:T(8,128)(2,1)S(1)}, bf16[256,1024]{1,0:T(8,128)(2,1)}, u32[]{:S(2)}) copy-start(bf16[256,1024]{1,0:T(8,128)(2,1)} %param.15) | copy-start | bytes 1572868
  590.0 144.9 %copy-start.3 = (f32[8,256]{1,0:T(8,128)S(1)}, f32[8,256]{1,0:T(8,128)}, u32[]{:S(2)}) copy-start(f32[8,256]{1,0:T(8,128)} %add_bitcast_fusion.1) | copy-start | bytes 24580
  733.1 19.4 %copy-start.4 = (f32[1024]{0:T(1024)S(1)}, f32[1024]{0:T(1024)}, u32[]{:S(2)}) copy-start(f32[1024]{0:T(1024)} %param.20) | copy-start | bytes 12292
Sparse Core Ops, SparseCore 0:
  12.3 600.2 all-gather.3
where the time goes:
time: 767 us; the launch traced here: 761 us
  blocking collectives  526 us (69%)
  other arithmetic  93.9 us (12%)
  local copies, waits for them, and re-layouts  64.9 us (8%)
  waiting for transfers between devices  21.6 us (3%)
  matrix products  20.6 us (3%)
  starting transfers between devices  19 us (2%)
  between operations  14.4 us (2%)
    all_gather x1, blocking collectives, entering_2(): everything = jax.tree.map(lambda part: lax.all_gather(part, axis), array)  511 us
    select_n x64, other arithmetic, turn(): return jax.tree.map(lambda a, b: jnp.where(reached, a, b), new, before)  75.1 us
    exp x64, local copies, waits for them, and re-layouts, combine_states(): jnp.exp(late_total)[:, None, None] * early_state + late_state  44.1 us
    all_gather x1, waiting for transfers between devices, entering_2(): everything = jax.tree.map(lambda part: lax.all_gather(part, axis), array)  21.6 us
    all_to_all x1, starting transfers between devices, cache_attention(): lax.all_to_all(outgoing, 'ctx', split_axis=0, concat_axis=0, tiled=True)  18.9 us
  transfers between devices with their start and end apart: 2, of which 1 were waited for; matrix products, arithmetic and copies ran while one was open for 6% of the time, Pallas kernels for 0%

commit v1 on v0

v1 whole, which is shorter than its diff:
```python
import functools
import math

import jax
import jax.numpy as jnp
from jax import lax
from jax.experimental import pallas as pl
from jax.experimental.pallas import tpu as pltpu
from jax.sharding import PartitionSpec as P

QUERY_HEADS = 64
HD = 128
BLOCK = 128
NZ = 16
NY = 4
MESH = pl.DeviceIdType.MESH
VMEM_LIMIT = 60 * 1024 * 1024


def exchange_kernel(sel_ref, ck_ref, cv_ref, st_ref, fin_ref, ent_ref, scr):
    bufs_p, bufs_m, far, stage = scr["bufs_p"], scr["bufs_m"], scr["far"], scr["stage"]
    me = lax.axis_index("ctx")
    z = me // NY
    y = me % NY

    def at(zz, yy):
        return {"ctx": zz * NY + yy}

    def zplus(k):
        return (z + k) % NZ

    def yplus(k):
        return (y + k) % NY

    barrier = pltpu.get_barrier_semaphore()
    for r in range(1, NY):
        pl.semaphore_signal(barrier, inc=1, device_id=at(z, yplus(r)), device_id_type=MESH)
    for r in range(1, NZ):
        pl.semaphore_signal(barrier, inc=1, device_id=at(zplus(r), y), device_id_type=MESH)
    pl.semaphore_wait(barrier, NY - 1 + NZ - 1)

    sends = []

    def copy(src, dst, ssem, rsem, where):
        made = pltpu.make_async_remote_copy(
            src_ref=src,
            dst_ref=dst,
            send_sem=ssem,
            recv_sem=rsem,
            device_id=where,
            device_id_type=MESH,
        )
        sends.append(made)
        return made

    yall, rz, tz, zr, zt = scr["yall"], scr["rz"], scr["tz"], scr["zr"], scr["zt"]
    ez, er, eq, pre = scr["ez"], scr["er"], scr["eq"], scr["pre"]
    ya = []
    for r in range(1, NY):
        ya.append(
            copy(
                st_ref.at[yplus(r)],
                yall.at[y],
                scr["ya_s"].at[r - 1],
                scr["ya_r"].at[r - 1],
                at(z, yplus(r)),
            )
        )
        ya[-1].start()
    def part(ref, c):
        return ref.at[c // 2, pl.ds(4 * (c % 2), 4)]

    def home(c):
        return (ck_ref, cv_ref)[c // 2].at[pl.ds(4 * (c % 2), 4)]

    def buffer(sign, d):
        if d == NZ // 2:
            return far
        return (bufs_p if sign > 0 else bufs_m)[d - 1]

    def travels(sign, d, c):
        return d < NZ // 2 or (d == NZ // 2 and (c < 2) == (sign > 0))

    ring = {}

    def send_ring(sign, d, c):
        if not travels(sign, d, c):
            return
        src = home(c) if d == 1 else part(buffer(sign, d - 1), c)
        k = 0 if sign > 0 else 1
        made = copy(
            src,
            part(buffer(sign, d), c),
            scr["ring_s"].at[k, d - 1, c],
            scr["ring_r"].at[k, d - 1, c],
            at(zplus(1 if sign > 0 else NZ - 1), y),
        )
        ring[sign, d, c] = made
        made.start()

    for c in range(4):
        send_ring(1, 1, c)
        send_ring(-1, 1, c)

    picks = []

    def pick(n, offset, load):
        source = zplus(offset) * NY + y
        for r in range(NY):
            spot = sel_ref[yplus(r), source]
            for kind in range(2):
                block = load(kind, spot)
                if r == 0:
                    fin_ref[source, kind] = block
                else:
                    stage[n, r - 1, kind] = block
        out = []
        for r in range(1, NY):
            out.append(
                copy(
                    stage.at[n, r - 1],
                    fin_ref.at[source],
                    scr["pick_s"].at[n, r - 1],
                    scr["pick_r"].at[n, r - 1],
                    at(z, yplus(r)),
                )
            )
        picks.extend(out)
        return out

    waiting = pick(0, 0, lambda kind, spot: (ck_ref, cv_ref)[kind][spot])

    hold = {}

    def row_totals():
        yall[y] = st_ref[y]
        for made in ya:
            made.wait_recv()
        for hh in range(2):
            rows = pl.ds(hh * HD, HD)
            total = jnp.zeros((1, HD), jnp.float32)
            state = jnp.zeros((HD, HD), jnp.float32)
            for k in range(NY):
                if k > 0:
                    pre[k, rows] = state
                    pre[k, pl.ds(2 * HD + hh, 1)] = total
                step = yall[k, pl.ds(2 * HD + hh, 1)]
                state = jnp.exp(step) * state + yall[k, rows]
                total = total + step
            tz[hh] = total
            rz[pl.ds(hh * 8, 8)] = state.astype(jnp.bfloat16).reshape(8, 16, HD)

    def send_totals():
        hold["za"] = []
        for r in range(1, NZ):
            to = zplus(r)
            one = copy(rz.at[to], zr.at[z], scr["za_s"].at[r - 1], scr["za_r"].at[r - 1], at(to, y))
            two = copy(
                tz.at[to // 8], zt.at[z], scr["zb_s"].at[r - 1], scr["zb_r"].at[r - 1], at(to, y)
            )
            one.start()
            two.start()
            hold["za"] += [one, two]
        zr[z] = rz[z]
        zt[z] = tz[z // 8]

    def scan():
        for made in hold["za"]:
            made.wait_recv()
        state = jnp.zeros((16, HD), jnp.float32)
        for k in range(NZ):
            ez[k] = state.astype(jnp.bfloat16)
            state = jnp.exp(zt[k]) * state + zr[k].astype(jnp.float32)

    def send_entering():
        hold["zc"] = []
        for r in range(1, NZ):
            to = zplus(r)
            one = copy(ez.at[to], er.at[z], scr["zc_s"].at[r - 1], scr["zc_r"].at[r - 1], at(to, y))
            one.start()
            hold["zc"].append(one)
        er[z] = ez[z]

    def members():
        for made in hold["zc"]:
            made.wait_recv()
        row = er[...].astype(jnp.float32).reshape(2 * HD, HD)
        eq[0] = row
        for k in range(1, NY):
            for hh in range(2):
                rows = pl.ds(hh * HD, HD)
                faded = jnp.exp(pre[k, pl.ds(2 * HD + hh, 1)]) * row[hh * HD : (hh + 1) * HD]
                eq[k, rows] = faded + pre[k, rows]

    def send_members():
        hold["yb"] = []
        for r in range(1, NY):
            to = yplus(r)
            one = copy(eq.at[to], ent_ref.at[y], scr["yb_s"].at[r - 1], scr["yb_r"].at[r - 1], at(z, to))
            one.start()
            hold["yb"].append(one)
        ent_ref[y] = eq[y]

    tasks = {
        (1, 0): row_totals,
        (1, 1): send_totals,
        (3, 1): scan,
        (3, 2): send_entering,
        (5, 1): members,
        (5, 2): send_members,
    }

    for d in range(1, NZ // 2 + 1):
        for c in range(4):
            for sign in (1, -1):
                if travels(sign, d, c):
                    ring[sign, d, c].wait_recv()
                if d < NZ // 2:
                    send_ring(sign, d + 1, c)
            if c == 0:
                for made in waiting:
                    made.start()
                waiting = []
            if (d, c) in tasks:
                tasks[d, c]()
        if d < NZ // 2:
            low, high = bufs_p[d - 1], bufs_m[d - 1]
            waiting = pick(2 * d - 1, NZ - d, lambda kind, spot, ref=low: ref[kind, spot])
            waiting += pick(2 * d, d, lambda kind, spot, ref=high: ref[kind, spot])
        else:
            waiting = pick(2 * d - 1, d, lambda kind, spot: far[kind, spot])
    for made in hold["yb"]:
        made.wait_recv()
    for made in waiting:
        made.start()
    for made in picks:
        made.wait_recv()
    for made in sends:
        made.wait_send()


def exchange(sel, ck, cv, st):
    names = {
        "bufs_p": [pltpu.VMEM((2, 8, BLOCK, HD), jnp.bfloat16)] * 7,
        "bufs_m": [pltpu.VMEM((2, 8, BLOCK, HD), jnp.bfloat16)] * 7,
        "far": pltpu.VMEM((2, 8, BLOCK, HD), jnp.bfloat16),
        "stage": pltpu.VMEM((NZ, NY - 1, 2, BLOCK, HD), jnp.bfloat16),
        "yall": pltpu.VMEM((NY, 264, HD), jnp.float32),
        "pre": pltpu.VMEM((NY, 264, HD), jnp.float32),
        "rz": pltpu.VMEM((NZ, 16, HD), jnp.bfloat16),
        "tz": pltpu.VMEM((2, 1, HD), jnp.float32),
        "zr": pltpu.VMEM((NZ, 16, HD), jnp.bfloat16),
        "zt": pltpu.VMEM((NZ, 1, HD), jnp.float32),
        "ez": pltpu.VMEM((NZ, 16, HD), jnp.bfloat16),
        "er": pltpu.VMEM((NZ, 16, HD), jnp.bfloat16),
        "eq": pltpu.VMEM((NY, 256, HD), jnp.float32),
        "ring_s": pltpu.SemaphoreType.DMA((2, 8, 4)),
        "ring_r": pltpu.SemaphoreType.DMA((2, 8, 4)),
        "pick_s": pltpu.SemaphoreType.DMA((NZ, NY - 1)),
        "pick_r": pltpu.SemaphoreType.DMA((NZ, NY - 1)),
        "ya_s": pltpu.SemaphoreType.DMA((NY - 1,)),
        "ya_r": pltpu.SemaphoreType.DMA((NY - 1,)),
        "yb_s": pltpu.SemaphoreType.DMA((NY - 1,)),
        "yb_r": pltpu.SemaphoreType.DMA((NY - 1,)),
        "za_s": pltpu.SemaphoreType.DMA((NZ - 1,)),
        "za_r": pltpu.SemaphoreType.DMA((NZ - 1,)),
        "zb_s": pltpu.SemaphoreType.DMA((NZ - 1,)),
        "zb_r": pltpu.SemaphoreType.DMA((NZ - 1,)),
        "zc_s": pltpu.SemaphoreType.DMA((NZ - 1,)),
        "zc_r": pltpu.SemaphoreType.DMA((NZ - 1,)),
    }
    flat, tree = jax.tree.flatten(names, is_leaf=lambda leaf: not isinstance(leaf, (dict, list)))

    def body(sel_ref, ck_ref, cv_ref, st_ref, fin_ref, ent_ref, *scratch):
        exchange_kernel(
            sel_ref, ck_ref, cv_ref, st_ref, fin_ref, ent_ref, jax.tree.unflatten(tree, scratch)
        )

    vmem = pl.BlockSpec(memory_space=pltpu.VMEM)
    return pl.pallas_call(
        body,
        out_shape=(
            jax.ShapeDtypeStruct((NZ * NY, 2, BLOCK, HD), jnp.bfloat16),
            jax.ShapeDtypeStruct((NY, 2 * HD, HD), jnp.float32),
        ),
        in_specs=[pl.BlockSpec(memory_space=pltpu.SMEM), vmem, vmem, vmem],
        out_specs=(vmem, vmem),
        scratch_shapes=flat,
        compiler_params=pltpu.CompilerParams(
            collective_id=0, has_side_effects=True, vmem_limit_bytes=VMEM_LIMIT
        ),
        name="exchange",
    )(sel, ck, cv, st)


NT = (((1,), (1,)), ((), ()))


def attend_kernel(src_ref, live_ref, q_ref, sk_ref, sv_ref, fin_ref, out_ref, qs, sc, top, tot, acc):
    factor = math.log2(math.e) / math.sqrt(HD)
    group = q_ref.shape[1] // HD
    rows = group * BLOCK
    chunk = 256

    for qb in range(2):
        tokens = pl.ds(qb * BLOCK, BLOCK)
        for g in range(group):
            qs[pl.ds(g * BLOCK, BLOCK)] = q_ref[tokens, g * HD : (g + 1) * HD]
        live = live_ref[qb]
        own = qb + 1

        def score(slot, keys, first=False, causal=False):
            for at in range(0, rows, chunk):
                part = pl.ds(at, chunk)
                s = lax.dot_general(qs[part], keys, NT, preferred_element_type=jnp.float32)
                if causal:
                    t = lax.broadcasted_iota(jnp.int32, (chunk, BLOCK), 0) % BLOCK
                    u = lax.broadcasted_iota(jnp.int32, (chunk, BLOCK), 1)
                    s = jnp.where(u <= t, s, -1e30)
                sc[slot, part] = s
                top[part] = s if first else jnp.maximum(top[part], s)

        score(0, sk_ref[tokens], first=True, causal=True)
        if qb == 1:
            score(1, sk_ref[pl.ds(0, BLOCK)])

        def more(j, carry):
            score(own + j, fin_ref[src_ref[qb, j], 0])
            return carry

        lax.fori_loop(0, live, more, 0)
        for at in range(0, rows, chunk):
            part = pl.ds(at, chunk)
            top[part] = jnp.broadcast_to(
                jnp.max(top[part], axis=1, keepdims=True) * factor, (chunk, BLOCK)
            )

        def mix(slot, values, first=False):
            for at in range(0, rows, chunk):
                part = pl.ds(at, chunk)
                w = jnp.exp2(sc[slot, part] * factor - top[part])
                m = jnp.dot(w.astype(jnp.bfloat16), values, preferred_element_type=jnp.float32)
                tot[part] = w if first else tot[part] + w
                acc[part] = m if first else acc[part] + m

        mix(0, sv_ref[tokens], first=True)
        if qb == 1:
            mix(1, sv_ref[pl.ds(0, BLOCK)])

        def again(j, carry):
            mix(own + j, fin_ref[src_ref[qb, j], 1])
            return carry

        lax.fori_loop(0, live, again, 0)
        for g in range(group):
            part = pl.ds(g * BLOCK, BLOCK)
            whole = jnp.sum(tot[part], axis=1, keepdims=True)
            out_ref[tokens, g * HD : (g + 1) * HD] = (acc[part] / whole).astype(jnp.bfloat16)


def attend(sources, live, queries, keys, values, fin):
    tok_rows, width = queries.shape
    rows = width // HD * BLOCK
    vmem = pl.BlockSpec(memory_space=pltpu.VMEM)
    smem = pl.BlockSpec(memory_space=pltpu.SMEM)
    return pl.pallas_call(
        attend_kernel,
        out_shape=jax.ShapeDtypeStruct((tok_rows, width), jnp.bfloat16),
        in_specs=[smem, smem, vmem, vmem, vmem, vmem],
        out_specs=vmem,
        scratch_shapes=[
            pltpu.VMEM((rows, HD), jnp.bfloat16),
            pltpu.VMEM((18, rows, BLOCK), jnp.float32),
            pltpu.VMEM((rows, BLOCK), jnp.float32),
            pltpu.VMEM((rows, BLOCK), jnp.float32),
            pltpu.VMEM((rows, HD), jnp.float32),
        ],
        compiler_params=pltpu.CompilerParams(vmem_limit_bytes=VMEM_LIMIT),
        name="attend",
    )(sources, live, queries, keys, values, fin)


def tables(block_lists, live_counts):
    place = lax.axis_index("ctx")
    selected = block_lists.shape[1]
    row = place // NY
    lists = lax.dynamic_slice_in_dim(block_lists, row * 2 * NY, 2 * NY, 0)
    counts = lax.dynamic_slice_in_dim(live_counts, row * 2 * NY, 2 * NY, 0)
    read = jnp.arange(selected, dtype=jnp.int32)[None, :] < counts[:, None]
    flat = jnp.where(read, lists, -1).reshape(NY, 2 * selected)
    owners = jnp.arange(NZ * NY, dtype=jnp.int32)
    hit = (flat >> 3)[:, :, None] == owners[None, None, :]
    sel = jnp.max(jnp.where(hit, (flat & 7)[:, :, None], 0), axis=1)
    mine = lax.dynamic_slice_in_dim(block_lists, place * 2, 2, 0) >> 3
    my_counts = lax.dynamic_slice_in_dim(live_counts, place * 2, 2, 0)
    return sel, mine, my_counts


def local(
    lin_queries,
    lin_keys,
    lin_values,
    log_decay,
    lin_gate,
    norm_gain,
    soft_queries,
    slab_keys,
    slab_values,
    cache_keys,
    cache_values,
    block_lists,
    live_counts,
):
    tok_rows = lin_queries.shape[0]
    head_count = lin_queries.shape[1] // HD
    sel, mine, my_counts = tables(block_lists, live_counts)
    act_queries = (
        jax.nn.silu(lin_queries.astype(jnp.float32))
        .astype(jnp.bfloat16)
        .reshape(tok_rows, head_count, HD)
    )
    act_keys = (
        jax.nn.silu(lin_keys.astype(jnp.float32))
        .astype(jnp.bfloat16)
        .reshape(tok_rows, head_count, HD)
    )
    values_here = lin_values.reshape(tok_rows, head_count, HD)
    running = jnp.cumsum(log_decay, axis=0)
    seg_total = running[-1]
    fade = jnp.exp(seg_total[None, :] - running)
    seg_state = jnp.einsum(
        "shd,she->hde",
        act_keys.astype(jnp.float32) * fade[:, :, None],
        values_here.astype(jnp.float32),
        precision=lax.Precision.HIGHEST,
    )
    st = jnp.concatenate(
        [
            seg_state.reshape(NY, 2 * HD, HD),
            jnp.broadcast_to(seg_total.reshape(NY, 2)[:, :, None], (NY, 2, HD)),
            jnp.zeros((NY, 6, HD), jnp.float32),
        ],
        axis=1,
    )
    blocks = cache_keys.shape[0] // BLOCK
    fin, entering = exchange(
        sel,
        cache_keys.reshape(blocks, BLOCK, HD),
        cache_values.reshape(blocks, BLOCK, HD),
        st,
    )
    entering = entering.reshape(head_count, HD, HD)
    soft_out = attend(mine, my_counts, soft_queries, slab_keys, slab_values, fin)

    flipped = running.T
    gaps = flipped[:, :, None] - flipped[:, None, :]
    causal = jnp.arange(tok_rows)[:, None] >= jnp.arange(tok_rows)[None, :]
    weight = jnp.where(causal[None], jnp.exp(jnp.minimum(gaps, 0.0)), 0.0)
    scores = jnp.einsum("thd,shd->hts", act_queries, act_keys, preferred_element_type=jnp.float32)
    lin_scores = (scores * weight).astype(jnp.bfloat16)
    intra = jnp.einsum("hts,shd->thd", lin_scores, values_here, preferred_element_type=jnp.float32)
    inter = jnp.exp(running)[:, :, None] * jnp.einsum(
        "thd,hde->the", act_queries.astype(jnp.float32), entering, precision=lax.Precision.HIGHEST
    )
    lin_attn = (intra + inter).reshape(tok_rows, head_count * HD)
    partial_squares = jnp.sum(lin_attn * lin_attn, axis=1)
    whole_squares = lax.psum(partial_squares, "head")
    scaling = lax.rsqrt(whole_squares / (QUERY_HEADS * HD) + 1e-06)
    gated = (
        lin_attn
        * scaling[:, None]
        * norm_gain[None, :]
        * jax.nn.sigmoid(lin_gate.astype(jnp.float32))
    )
    return (gated.astype(jnp.bfloat16), soft_out)


def solution(mesh):
    in_specs = (
        P("ctx", "head"),
        P("ctx", "head"),
        P("ctx", "head"),
        P("ctx", "head"),
        P("ctx", "head"),
        P("head"),
        P("ctx", "head"),
        P("ctx", "head"),
        P("ctx", "head"),
        P("ctx", "head"),
        P("ctx", "head"),
        P(),
        P(),
    )
    out_specs = (P("ctx", "head"), P("ctx", "head"))
    return jax.shard_map(local, mesh=mesh, in_specs=in_specs, out_specs=out_specs, check_vma=False)
```

time: 767 us -> 168 us (0.22)
  blocking collectives: 526 us -> 12.5 us
  Pallas kernels: 0 us -> 139 us
  other arithmetic: 93.9 us -> 6.27 us
  local copies, waits for them, and re-layouts: 64.9 us -> 3.7 us
  waiting for transfers between devices: 21.6 us -> 0 us
  starting transfers between devices: 19 us -> 0 us
  matrix products: 20.6 us -> 5.86 us
  between operations: 14.4 us -> 0.77 us
    all_gather x1 -> x0, blocking collectives: 511 us -> none  [entering_2(): everything = jax.tree.map(lambda part: lax.all_gather(part, axis), array)]
    pallas_call x0 -> x2, Pallas kernels: none -> 139 us  [the longest x1 119 us: exchange(): pl.pallas_call(body, out_shape=(jax.ShapeDtypeStruct((NZ * NY, 2, BLOCK,...]
    select_n x65 -> x0, other arithmetic: 75.8 us -> none  [the longest x64 75.1 us: turn(): return jax.tree.map(lambda a, b: jnp.where(reached, a, b), new, before)]
    exp x64 -> x0, local copies, waits for them, and re-layouts: 44.1 us -> none  [combine_states(): jnp.exp(late_total)[:, None, None] * early_state + late_state]
    all_gather x1 -> x0, waiting for transfers between devices: 21.6 us -> none  [entering_2(): everything = jax.tree.map(lambda part: lax.all_gather(part, axis), array)]
    all_to_all x1 -> x0, starting transfers between devices: 18.9 us -> none  [cache_attention(): lax.all_to_all(outgoing, 'ctx', split_axis=0, concat_axis=0, tiled=True)]
    dot_general x8 -> x3, matrix products: 20.6 us -> 5.86 us  [the longest x1 2.82 us: local(): jnp.einsum('thd,hde->the', act_queries.astype(jnp.float32), entering, pre...]
    unnamed x22 -> x14, local copies, waits for them, and re-layouts: 10.4 us -> 0.19 us
  transfers between devices with their start and end apart: 2 -> 0, of which waited for: 1 -> 0; matrix products, arithmetic and copies ran while one was open for 6% -> 0% of each run, Pallas kernels for 0% -> 0%
where the time goes in v1:
time: 168 us
  Pallas kernels  139 us (83%)
  blocking collectives  12.5 us (7%)
  other arithmetic  6.27 us (4%)
  matrix products  5.86 us (3%)
  local copies, waits for them, and re-layouts  3.7 us (2%)
    pallas_call x1, Pallas kernels, exchange(): pl.pallas_call(body, out_shape=(jax.ShapeDtypeStruct((NZ * NY, 2, BLOCK,...  119 us
    pallas_call x1, Pallas kernels, attend(): pl.pallas_call(attend_kernel, out_shape=jax.ShapeDtypeStruct((tok_rows, w...  19.7 us
    psum x1, blocking collectives, local(): whole_squares = lax.psum(partial_squares, 'head')  12.5 us

profile of v1, /device:TPU:16, one launch (start us, length us, event | category | flops | bytes accessed | tf_op | source)
XLA Modules:
  0.0 167.9 jit_solution(7838924659561058926)
XLA Ops:
  0.6 0.0 copy-start
  0.7 0.8 constant_dynamic-slice_fusion.1
  1.5 0.1 copy.70
  1.6 0.7 dynamic_slice.12
  2.3 0.1 fusion.33
  2.4 0.1 and.22
  2.4 0.1 shift_right_arithmetic.21
  2.5 0.7 select_reduce_fusion.sel_ref
  3.2 1.2 reduce-window.6
  4.5 0.2 slice_reduce_fusion
  4.7 0.1 fusion.35
  4.7 0.2 slice_reduce_fusion.1
  4.9 0.1 subtract_exponential_fusion
  5.0 1.4 fusion.11
  6.4 0.2 copy.72
  6.6 0.0 copy-start.4
  6.6 0.0 copy-done
  6.6 0.7 fusion.12
  7.3 0.1 broadcast_in_dim.54
  7.4 0.1 broadcast_in_dim.55
  7.5 0.1 pad.2.clone
  7.5 0.9 maximum_maximum_fusion.st_ref
  8.5 119.1 %exchange.1 = (bf16[64,2,128,128]{3,2,1,0:T(8,128)(2,1)}, f32[4,256,128]{2,1,0:T(8,128)}) custom-call(s32[4,64]{1,0:T(4,128)} %select_reduce_fusion.sel_ref, bf16[8,128,128]{2,1,0:T(8,128)(2,1)} %bitcast.58, bf16[8,128,128]{2,1,0:T(8,128)(2,1)} %bitcast.59, f32[4,264,128]{2,1,0:T(8,128)} %maximum_maximum_fusion.st_ref), custom_call_target="tpu_custom_call" | custom-call | tf_op jit(solution)/shard_map/exchange/pallas_call | solution.py:280
  127.6 0.0 copy-done.4
  127.6 2.8 %fusion.3 = f32[256,8,128]{0,2,1:T(8,128)} fusion(f32[8,128,128]{2,1,0:T(8,128)} %bitcast.61, f32[256,8]{0,1:T(8,128)S(1)} %get-tuple-element.6, bf16[256,1024]{1,0:T(8,128)(2,1)S(1)} %copy-done.4), kind=kOutput, calls=%fused_computation.5 | convolution fusion | flops 404488192 | bytes 2105344 | tf_op jit(solution)/shard_map/thd,hde->the/dot_general | solution.py:462
  130.4 0.1 add_bitcast_fusion.1
  130.5 2.3 %multiply_reduce_fusion = (f32[256]{0:T(256)S(1)}, f32[256,8,128]{0,2,1:T(8,128)S(1)}) fusion(f32[256,8,128]{0,2,1:T(8,128)} %fusion.3, bf16[256,8,128]{0,2,1:T(8,128)(2,1)S(1)} %bitcast.55, f32[8,256]{1,0:T(8,128)S(1)} %add_bitcast_fusion.1, pred[256,256]{1,0:T(8,128)(4,1)S(1)} %iota_compare_fusion, bf16[256,1024]{1,0:T(8,128)(2,1)S(1)} %copy-done, ...), kind=kOutput, calls=%fused_computation.19 | convolution fusion | flops 273415936 | bytes 3744768 | tf_op jit(solution)/shard_map/hts,shd->thd/dot_general | solution.py:461
  132.8 0.0 copy-start.1
  132.8 0.0 copy-start.3
  132.9 0.0 copy-start.2
  132.9 0.0 copy-start.5
  132.9 0.3 copy.67
  133.2 12.5 %psum.7 = f32[256]{0:T(256)S(1)} all-reduce(f32[256]{0:T(256)S(1)} %get-tuple-element.10), channel_id=1, replica_groups=mesh['ctx'=64,'head'=8] {'head'}, use_global_device_ids=true, to_apply=%region_4.5 | all-reduce | flops 256 | bytes 2048 | tf_op jit(solution)/shard_map/psum | solution.py:467
  145.7 0.0 copy-done.1
  145.7 0.0 copy-done.3
  145.8 1.1 multiply_convert_fusion.1
  146.9 0.0 copy-done.2
  146.9 0.1 constant_dynamic-slice_fusion
  146.9 0.1 copy.71
  147.0 0.6 broadcast_shift-right-arithmetic_fusion.src_ref
  147.6 0.0 copy-done.5
  147.6 0.6 dynamic_slice.15.live_ref
  148.2 19.7 %attend.1 = bf16[256,1024]{1,0:T(8,128)(2,1)} custom-call(s32[2,16]{1,0:T(2,128)} %broadcast_shift-right-arithmetic_fusion.src_ref, s32[2]{0:T(128)} %dynamic_slice.15.live_ref, bf16[256,1024]{1,0:T(8,128)(2,1)} %q_ref.1, bf16[256,128]{1,0:T(8,128)(2,1)} %sk_ref.1, bf16[256,128]{1,0:T(8,128)(2,1)} %sv_ref.1, bf16[64,2,128,128]{3,2,1,0:T(8,128)(2,1)} %get-tuple-element.5.fin_ref), custom_call_target="tpu_custom_call" | custom-call | tf_op jit(solution)/shard_map/attend/pallas_call | solution.py:366
  (5 shorter events, 0.1 us)
Async XLA Ops:
  0.6 6.0 %copy-start = (bf16[256,1024]{1,0:T(8,128)(2,1)S(1)}, bf16[256,1024]{1,0:T(8,128)(2,1)}, u32[]{:S(2)}) copy-start(bf16[256,1024]{1,0:T(8,128)(2,1)} %param.15) | copy-start | bytes 1572868
  6.6 121.0 %copy-start.4 = (bf16[256,1024]{1,0:T(8,128)(2,1)S(1)}, bf16[256,1024]{1,0:T(8,128)(2,1)}, u32[]{:S(2)}) copy-start(bf16[256,1024]{1,0:T(8,128)(2,1)} %param.13) | copy-start | bytes 1572868
  132.8 12.9 %copy-start.1 = (bf16[256,1024]{1,0:T(8,128)(2,1)S(1)}, bf16[256,1024]{1,0:T(8,128)(2,1)}, u32[]{:S(2)}) copy-start(bf16[256,1024]{1,0:T(8,128)(2,1)} %param.17) | copy-start | bytes 1572868
  132.8 12.9 %copy-start.3 = (f32[1024]{0:T(1024)S(1)}, f32[1024]{0:T(1024)}, u32[]{:S(2)}) copy-start(f32[1024]{0:T(1024)} %param.18) | copy-start | bytes 12292
  132.9 14.0 %copy-start.2 = (s32[128,16]{0,1:T(8,128)S(1)}, s32[128,16]{0,1:T(8,128)}, u32[]{:S(2)}) copy-start(s32[128,16]{0,1:T(8,128)} %param.24) | copy-start | bytes 24580
  132.9 14.7 %copy-start.5 = (s32[128]{0:T(128)S(1)}, s32[128]{0:T(128)}, u32[]{:S(2)}) copy-start(s32[128]{0:T(128)} %param.25) | copy-start | bytes 1540

commit v2 on v1

v2 whole, which is shorter than its diff:
```python
import functools
import math

import jax
import jax.numpy as jnp
from jax import lax
from jax.experimental import pallas as pl
from jax.experimental.pallas import tpu as pltpu
from jax.sharding import PartitionSpec as P

QUERY_HEADS = 64
HD = 128
BLOCK = 128
NZ = 16
NY = 4
MESH = pl.DeviceIdType.MESH
VMEM_LIMIT = 60 * 1024 * 1024


NT = (((1,), (1,)), ((), ()))
TN = (((0,), (0,)), ((), ()))
LAST = 6
HIGHEST = lax.Precision.HIGHEST


def exchange_kernel(
    sel_ref, ck_ref, cv_ref, lq_ref, lk_ref, lv_ref, lg_ref, ld_ref, gain_ref, fin_ref, lin_ref, scr
):
    me = lax.axis_index("ctx")
    mine = lax.axis_index("head")
    z = me // NY
    y = me % NY
    heads = 2 * NY

    def zplus(k):
        return (z + k) % NZ

    def yplus(k):
        return (y + k) % NY

    def at(zz, yy):
        return {"ctx": zz * NY + yy, "head": mine}

    def beside(r):
        return {"ctx": me, "head": (mine + r) % heads}

    sends = []

    def copy(src, dst, ssem, rsem, where):
        made = pltpu.make_async_remote_copy(
            src_ref=src,
            dst_ref=dst,
            send_sem=ssem,
            recv_sem=rsem,
            device_id=where,
            device_id_type=MESH,
        )
        sends.append(made)
        return made

    lq, lk, lv, lg, own_k, own_v = (scr[n] for n in ("lq", "lk", "lv", "lg", "own_k", "own_v"))
    loads = {}
    for n, (name, src, dst) in enumerate(
        (
            ("k", lk_ref, lk),
            ("v", lv_ref, lv),
            ("ck", ck_ref, own_k),
            ("cv", cv_ref, own_v),
            ("q", lq_ref, lq),
            ("g", lg_ref, lg),
        )
    ):
        loads[name] = pltpu.make_async_copy(src, dst, scr["in_s"].at[n])
        loads[name].start()

    barrier = pltpu.get_barrier_semaphore()
    friends = [at(z, yplus(r)) for r in range(1, NY)]
    friends += [at(zplus(r), y) for r in range(1, NZ)]
    friends += [at(zplus(k), yplus(r)) for k in (1, 2, NZ - 1, NZ - 2) for r in range(1, NY)]
    friends += [beside(r) for r in range(1, heads)]
    for friend in friends:
        pl.semaphore_signal(barrier, inc=1, device_id=friend, device_id_type=MESH)
    pl.semaphore_wait(barrier, len(friends))

    bufs = {
        (sign, d): scr["bufs"][2 * (2 * (d - 1) + (sign < 0)) :][:2]
        for d in range(1, LAST + 1)
        for sign in (1, -1)
    }
    ring = {}

    def send_ring(sign, d, c):
        half = pl.ds(4 * (c % 2), 4)
        src = (ck_ref, cv_ref)[c // 2] if d == 1 else bufs[sign, d - 1][c // 2]
        k = 0 if sign > 0 else 1
        made = copy(
            src.at[half],
            bufs[sign, d][c // 2].at[half],
            scr["ring_s"].at[k, d - 1, c],
            scr["ring_r"].at[k, d - 1, c],
            at(zplus(1 if sign > 0 else NZ - 1), y),
        )
        ring[sign, d, c] = made
        made.start()

    for c in range(4):
        send_ring(1, 1, c)
        send_ring(-1, 1, c)

    decay = ld_ref[...]
    tokens = decay.shape[0]
    row_id = lax.broadcasted_iota(jnp.int32, (tokens, tokens), 0)
    col_id = lax.broadcasted_iota(jnp.int32, (tokens, tokens), 1)
    triangle = jnp.where(col_id <= row_id, 1.0, 0.0).astype(jnp.float32)
    down_all = scr["down"]
    down_all[...] = lax.dot_general(
        triangle, decay, (((1,), (0,)), ((), ())), precision=HIGHEST, preferred_element_type=jnp.float32
    )
    across_all = scr["across"]
    across_all[...] = lax.dot_general(
        decay, triangle, (((0,), (1,)), ((), ())), precision=HIGHEST, preferred_element_type=jnp.float32
    )

    def silu(u):
        return u / (1.0 + jnp.exp(-u))

    def lanes(h):
        return slice(h * HD, (h + 1) * HD)

    st = scr["st"]
    loads["k"].wait()
    loads["v"].wait()
    for h in range(heads):
        down = down_all[:, h : h + 1]
        total = down[tokens - 1 : tokens]
        key = silu(lk[:, lanes(h)].astype(jnp.float32)).astype(jnp.bfloat16)
        lk[:, lanes(h)] = key
        faded = key.astype(jnp.float32) * jnp.exp(total - down)
        high = faded.astype(jnp.bfloat16)
        low = (faded - high.astype(jnp.float32)).astype(jnp.bfloat16)
        value = lv[:, lanes(h)]
        state = lax.dot_general(high, value, TN, preferred_element_type=jnp.float32)
        state += lax.dot_general(low, value, TN, preferred_element_type=jnp.float32)
        st[h // 2, pl.ds((h % 2) * HD, HD)] = state
        st[h // 2, pl.ds(2 * HD + h % 2, 1)] = jnp.broadcast_to(total, (1, HD))

    yall, rz, tz, zr, zt = scr["yall"], scr["rz"], scr["tz"], scr["zr"], scr["zt"]
    ez, er, eq, pre, ent = scr["ez"], scr["er"], scr["eq"], scr["pre"], scr["ent"]

    stage, far = scr["stage"], scr["far"]
    picks = []

    def pick(n, offset, refs, kinds):
        source = zplus(offset) * NY + y
        for r in range(NY):
            spot = sel_ref[z * NY + yplus(r), source]
            for kind in kinds:
                block = refs[kind][spot]
                if r == 0:
                    fin_ref[source, kind] = block
                else:
                    stage[n, r - 1, kind] = block
        out = []
        for r in range(1, NY):
            for kind in kinds if len(kinds) == 1 else (None,):
                a, b, c = stage.at[n, r - 1], fin_ref.at[source], 0
                if kind is not None:
                    a, b, c = a.at[kind], b.at[kind], kind
                out.append(
                    copy(
                        a,
                        b,
                        scr["pick_s"].at[n, r - 1, c],
                        scr["pick_r"].at[n, r - 1, c],
                        at(z, yplus(r)),
                    )
                )
        picks.extend(out)
        return out

    def pick_far(sign, kind):
        k = 0 if sign > 0 else 1
        source = zplus(NZ - LAST * sign) * NY + y
        out = []
        for beyond in (1, 2):
            to = zplus(NZ + sign * beyond)
            for r in range(NY):
                if beyond == 2 and (r < 2) != (sign > 0):
                    continue
                spot = sel_ref[to * NY + yplus(r), source]
                far[k, beyond - 1, r, kind] = bufs[sign, LAST][kind][spot]
                out.append(
                    copy(
                        far.at[k, beyond - 1, r, kind],
                        fin_ref.at[source, kind],
                        scr["far_s"].at[k, beyond - 1, r, kind],
                        scr["far_r"].at[k, beyond - 1, r, kind],
                        at(to, yplus(r)),
                    )
                )
        picks.extend(out)
        return out

    hold = {}

    def send_states():
        hold["ya"] = []
        for r in range(1, NY):
            made = copy(
                st.at[yplus(r)],
                yall.at[y],
                scr["ya_s"].at[r - 1],
                scr["ya_r"].at[r - 1],
                at(z, yplus(r)),
            )
            made.start()
            hold["ya"].append(made)

    def row_totals():
        yall[y] = st[y]
        for made in hold["ya"]:
            made.wait_recv()
        for hh in range(2):
            rows = pl.ds(hh * HD, HD)
            total = jnp.zeros((1, HD), jnp.float32)
            state = jnp.zeros((HD, HD), jnp.float32)
            for k in range(NY):
                if k > 0:
                    pre[k, rows] = state
                    pre[k, pl.ds(2 * HD + hh, 1)] = total
                step = yall[k, pl.ds(2 * HD + hh, 1)]
                state = jnp.exp(step) * state + yall[k, rows]
                total = total + step
            tz[hh] = total
            rz[pl.ds(hh * 8, 8)] = state.astype(jnp.bfloat16).reshape(8, 16, HD)

    def send_totals():
        hold["za"] = []
        for r in range(1, NZ):
            to = zplus(r)
            one = copy(rz.at[to], zr.at[z], scr["za_s"].at[r - 1], scr["za_r"].at[r - 1], at(to, y))
            two = copy(
                tz.at[to // 8], zt.at[z], scr["zb_s"].at[r - 1], scr["zb_r"].at[r - 1], at(to, y)
            )
            one.start()
            two.start()
            hold["za"] += [one, two]
        zr[z] = rz[z]
        zt[z] = tz[z // 8]

    def scan():
        for made in hold["za"]:
            made.wait_recv()
        state = jnp.zeros((16, HD), jnp.float32)
        for k in range(NZ):
            ez[k] = state.astype(jnp.bfloat16)
            state = jnp.exp(zt[k]) * state + zr[k].astype(jnp.float32)

    def send_entering():
        hold["zc"] = []
        for r in range(1, NZ):
            to = zplus(r)
            one = copy(ez.at[to], er.at[z], scr["zc_s"].at[r - 1], scr["zc_r"].at[r - 1], at(to, y))
            one.start()
            hold["zc"].append(one)
        er[z] = ez[z]

    def members():
        for made in hold["zc"]:
            made.wait_recv()
        row = er[...].astype(jnp.float32).reshape(2 * HD, HD)
        eq[0] = row
        for k in range(1, NY):
            for hh in range(2):
                rows = pl.ds(hh * HD, HD)
                faded = jnp.exp(pre[k, pl.ds(2 * HD + hh, 1)]) * row[hh * HD : (hh + 1) * HD]
                eq[k, rows] = faded + pre[k, rows]

    def send_members():
        hold["yb"] = []
        for r in range(1, NY):
            to = yplus(r)
            one = copy(eq.at[to], ent.at[y], scr["yb_s"].at[r - 1], scr["yb_r"].at[r - 1], at(z, to))
            one.start()
            hold["yb"].append(one)
        ent[y] = eq[y]

    attn = scr["attn"]

    def intra(h):
        if h == 0:
            loads["q"].wait()
        query = silu(lq[:, lanes(h)].astype(jnp.float32)).astype(jnp.bfloat16)
        lq[:, lanes(h)] = query
        scores = lax.dot_general(query, lk[:, lanes(h)], NT, preferred_element_type=jnp.float32)
        gaps = down_all[:, h : h + 1] - across_all[h : h + 1, :]
        t = lax.broadcasted_iota(jnp.int32, (tokens, tokens), 0)
        u = lax.broadcasted_iota(jnp.int32, (tokens, tokens), 1)
        weight = jnp.where(u <= t, jnp.exp(jnp.minimum(gaps, 0.0)), 0.0)
        attn[:, lanes(h)] = jnp.dot(
            (scores * weight).astype(jnp.bfloat16), lv[:, lanes(h)], preferred_element_type=jnp.float32
        )

    squares, norms = scr["squares"], scr["norms"]

    def inter(h):
        state = ent[h // 2, pl.ds((h % 2) * HD, HD)]
        high = state.astype(jnp.bfloat16)
        low = (state - high.astype(jnp.float32)).astype(jnp.bfloat16)
        query = lq[:, lanes(h)]
        moved = jnp.dot(query, high, preferred_element_type=jnp.float32)
        moved += jnp.dot(query, low, preferred_element_type=jnp.float32)
        whole = attn[:, lanes(h)] + jnp.exp(down_all[:, h : h + 1]) * moved
        attn[:, lanes(h)] = whole
        squares[...] = whole * whole if h == 0 else squares[...] + whole * whole

    def send_squares():
        norms[0] = lax.dot_general(
            jnp.ones((8, HD), jnp.float32),
            squares[...],
            NT,
            precision=HIGHEST,
            preferred_element_type=jnp.float32,
        )

    def start_squares():
        hold["sq"] = []
        for r in range(1, heads):
            one = copy(
                norms.at[0], norms.at[r], scr["sq_s"].at[r - 1], scr["sq_r"].at[r - 1], beside(r)
            )
            one.start()
            hold["sq"].append(one)

    def gate():
        for made in hold["sq"]:
            made.wait_recv()
        summed = norms[0]
        for r in range(1, heads):
            summed = summed + norms[r]
        first = jnp.where(lax.broadcasted_iota(jnp.int32, (8, HD), 0) == 0, 1.0, 0.0)
        tall = lax.dot_general(
            summed,
            first.astype(jnp.float32),
            TN,
            precision=HIGHEST,
            preferred_element_type=jnp.float32,
        )
        scaling = lax.rsqrt(tall / (QUERY_HEADS * HD) + 1e-06)
        loads["g"].wait()
        for h in range(heads):
            opened = 1.0 + jnp.exp(-lg[:, lanes(h)].astype(jnp.float32))
            shaped = attn[:, lanes(h)] * scaling * gain_ref[:, lanes(h)]
            lin_ref[:, lanes(h)] = (shaped / opened).astype(jnp.bfloat16)

    loads["ck"].wait()
    loads["cv"].wait()
    send_states()
    waiting = pick(0, 0, (own_k, own_v), (0, 1))
    tasks = {
        (1, 2): [row_totals],
        (1, 3): [send_totals],
        (2, 0): [lambda: intra(0)],
        (2, 1): [lambda: intra(1)],
        (2, 2): [lambda: intra(2)],
        (2, 3): [lambda: intra(3)],
        (3, 1): [scan],
        (3, 2): [send_entering],
        (4, 0): [lambda: intra(4)],
        (4, 1): [lambda: intra(5)],
        (4, 2): [lambda: intra(6)],
        (4, 3): [lambda: intra(7)],
        (5, 1): [members],
        (5, 2): [send_members],
    }
    for d in range(1, LAST + 1):
        for c in range(4):
            for sign in (1, -1):
                ring[sign, d, c].wait_recv()
                if d < LAST:
                    send_ring(sign, d + 1, c)
            for made in waiting:
                made.start()
            waiting = []
            for task in tasks.get((d, c), []):
                task()
            if d == LAST and c % 2 == 1:
                kind = c // 2
                waiting = pick_far(1, kind) + pick_far(-1, kind)
                waiting += pick(2 * d - 1, NZ - d, bufs[1, d], (kind,))
                waiting += pick(2 * d, d, bufs[-1, d], (kind,))
        if d < LAST:
            waiting = pick(2 * d - 1, NZ - d, bufs[1, d], (0, 1))
            waiting += pick(2 * d, d, bufs[-1, d], (0, 1))
    for made in waiting:
        made.start()
    for made in hold["yb"]:
        made.wait_recv()
    for h in range(heads):
        inter(h)
    send_squares()
    start_squares()
    gate()
    for made in picks:
        made.wait_recv()
    for made in sends:
        made.wait_send()


def exchange(sel, ck, cv, lq, lk, lv, lg, ld, gain):
    tokens, width = lq.shape
    shards = 2 * LAST + 1
    dma = pltpu.SemaphoreType.DMA
    names = {
        "bufs": [pltpu.VMEM((8, BLOCK, HD), jnp.bfloat16)] * (4 * LAST),
        "own_k": pltpu.VMEM((8, BLOCK, HD), jnp.bfloat16),
        "own_v": pltpu.VMEM((8, BLOCK, HD), jnp.bfloat16),
        "stage": pltpu.VMEM((shards, NY - 1, 2, BLOCK, HD), jnp.bfloat16),
        "far": pltpu.VMEM((2, 2, NY, 2, BLOCK, HD), jnp.bfloat16),
        "lq": pltpu.VMEM((tokens, width), jnp.bfloat16),
        "lk": pltpu.VMEM((tokens, width), jnp.bfloat16),
        "lv": pltpu.VMEM((tokens, width), jnp.bfloat16),
        "lg": pltpu.VMEM((tokens, width), jnp.bfloat16),
        "attn": pltpu.VMEM((tokens, width), jnp.float32),
        "squares": pltpu.VMEM((tokens, HD), jnp.float32),
        "norms": pltpu.VMEM((8, 8, tokens), jnp.float32),
        "down": pltpu.VMEM((tokens, 8), jnp.float32),
        "across": pltpu.VMEM((8, tokens), jnp.float32),
        "st": pltpu.VMEM((NY, 264, HD), jnp.float32),
        "yall": pltpu.VMEM((NY, 264, HD), jnp.float32),
        "pre": pltpu.VMEM((NY, 264, HD), jnp.float32),
        "rz": pltpu.VMEM((NZ, 16, HD), jnp.bfloat16),
        "tz": pltpu.VMEM((2, 1, HD), jnp.float32),
        "zr": pltpu.VMEM((NZ, 16, HD), jnp.bfloat16),
        "zt": pltpu.VMEM((NZ, 1, HD), jnp.float32),
        "ez": pltpu.VMEM((NZ, 16, HD), jnp.bfloat16),
        "er": pltpu.VMEM((NZ, 16, HD), jnp.bfloat16),
        "eq": pltpu.VMEM((NY, 256, HD), jnp.float32),
        "ent": pltpu.VMEM((NY, 256, HD), jnp.float32),
        "in_s": dma((6,)),
        "ring_s": dma((2, LAST, 4)),
        "ring_r": dma((2, LAST, 4)),
        "pick_s": dma((shards, NY - 1, 2)),
        "pick_r": dma((shards, NY - 1, 2)),
        "far_s": dma((2, 2, NY, 2)),
        "far_r": dma((2, 2, NY, 2)),
        "ya_s": dma((NY - 1,)),
        "ya_r": dma((NY - 1,)),
        "yb_s": dma((NY - 1,)),
        "yb_r": dma((NY - 1,)),
        "za_s": dma((NZ - 1,)),
        "za_r": dma((NZ - 1,)),
        "zb_s": dma((NZ - 1,)),
        "zb_r": dma((NZ - 1,)),
        "zc_s": dma((NZ - 1,)),
        "zc_r": dma((NZ - 1,)),
        "sq_s": dma((7,)),
        "sq_r": dma((7,)),
    }
    flat, tree = jax.tree.flatten(names, is_leaf=lambda leaf: not isinstance(leaf, (dict, list)))

    def body(*refs):
        exchange_kernel(*refs[:11], jax.tree.unflatten(tree, refs[11:]))

    vmem = pl.BlockSpec(memory_space=pltpu.VMEM)
    hbm = pl.BlockSpec(memory_space=pl.ANY)
    return pl.pallas_call(
        body,
        out_shape=(
            jax.ShapeDtypeStruct((NZ * NY, 2, BLOCK, HD), jnp.bfloat16),
            jax.ShapeDtypeStruct((tokens, width), jnp.bfloat16),
        ),
        in_specs=[pl.BlockSpec(memory_space=pltpu.SMEM)] + [hbm] * 6 + [vmem] * 2,
        out_specs=(vmem, vmem),
        scratch_shapes=flat,
        compiler_params=pltpu.CompilerParams(
            collective_id=0, has_side_effects=True, vmem_limit_bytes=VMEM_LIMIT
        ),
        name="exchange",
    )(sel, ck, cv, lq, lk, lv, lg, ld, gain)


GROUP = 4


def attend_kernel(lists_ref, counts_ref, q_ref, sk_ref, sv_ref, fin_ref, out_ref, qs, keys, values, sc, top, tot, acc):
    me = lax.axis_index("ctx")
    factor = math.log2(math.e) / math.sqrt(HD)
    heads = q_ref.shape[1] // HD
    selected = lists_ref.shape[1]
    rows = heads * BLOCK
    chunk = BLOCK
    wide = GROUP * BLOCK

    def parts(full):
        return [full[:, i * BLOCK : (i + 1) * BLOCK] for i in range(GROUP)]

    for qb in range(2):
        tokens = pl.ds(qb * BLOCK, BLOCK)
        query_block = 2 * me + qb
        own = qb + 1
        for g in range(heads):
            qs[pl.ds(g * BLOCK, BLOCK)] = q_ref[tokens, g * HD : (g + 1) * HD]
        keys[0:BLOCK] = sk_ref[tokens]
        values[0:BLOCK] = sv_ref[tokens]
        if qb == 1:
            keys[BLOCK : 2 * BLOCK] = sk_ref[0:BLOCK]
            values[BLOCK : 2 * BLOCK] = sv_ref[0:BLOCK]
        for j in range(selected):
            source = lists_ref[query_block, j] >> 3
            place = pl.ds((own + j) * BLOCK, BLOCK)
            keys[place] = fin_ref[source, 0]
            values[place] = fin_ref[source, 1]
        if own + selected < 5 * GROUP:
            place = pl.ds((own + selected) * BLOCK, (5 * GROUP - own - selected) * BLOCK)
            keys[place] = jnp.zeros(((5 * GROUP - own - selected) * BLOCK, HD), jnp.bfloat16)
            values[place] = jnp.zeros(((5 * GROUP - own - selected) * BLOCK, HD), jnp.bfloat16)
        filled = (own + counts_ref[query_block]) * BLOCK

        def score(n, first):
            base = 0 if first else pl.multiple_of(n * wide, wide)
            these = keys[pl.ds(base, wide)]
            for at in range(0, rows, chunk):
                part = pl.ds(at, chunk)
                s = lax.dot_general(qs[part], these, NT, preferred_element_type=jnp.float32)
                u = lax.broadcasted_iota(jnp.int32, (chunk, wide), 1)
                keep = u < filled - base
                if first:
                    t = lax.broadcasted_iota(jnp.int32, (chunk, wide), 0)
                    keep = keep & ((u <= t) | (u >= BLOCK))
                s = jnp.where(keep, s, -1e30)
                sc[n, part] = s
                most = functools.reduce(jnp.maximum, parts(s))
                top[part] = most if first else jnp.maximum(top[part], most)

        def mix(n, first):
            base = 0 if first else pl.multiple_of(n * wide, wide)
            these = values[pl.ds(base, wide)]
            for at in range(0, rows, chunk):
                part = pl.ds(at, chunk)
                peak = top[part]
                w = [jnp.exp2(s * factor - peak) for s in parts(sc[n, part])]
                m = jnp.dot(
                    jnp.concatenate([piece.astype(jnp.bfloat16) for piece in w], axis=1),
                    these,
                    preferred_element_type=jnp.float32,
                )
                some = functools.reduce(jnp.add, w)
                tot[part] = some if first else tot[part] + some
                acc[part] = m if first else acc[part] + m

        def body(step):
            def run(n, carry):
                step(n, False)
                return carry

            return run

        groups = (filled + wide - 1) // wide
        score(0, True)
        lax.fori_loop(1, groups, body(score), 0)
        for at in range(0, rows, chunk):
            part = pl.ds(at, chunk)
            top[part] = jnp.broadcast_to(
                jnp.max(top[part], axis=1, keepdims=True) * factor, (chunk, BLOCK)
            )
        mix(0, True)
        lax.fori_loop(1, groups, body(mix), 0)
        for g in range(heads):
            part = pl.ds(g * BLOCK, BLOCK)
            whole = jnp.sum(tot[part], axis=1, keepdims=True)
            out_ref[tokens, g * HD : (g + 1) * HD] = (acc[part] / whole).astype(jnp.bfloat16)


def attend(lists, counts, queries, keys, values, fin):
    tok_rows, width = queries.shape
    rows = width // HD * BLOCK
    vmem = pl.BlockSpec(memory_space=pltpu.VMEM)
    smem = pl.BlockSpec(memory_space=pltpu.SMEM)
    return pl.pallas_call(
        attend_kernel,
        out_shape=jax.ShapeDtypeStruct((tok_rows, width), jnp.bfloat16),
        in_specs=[smem, smem, vmem, vmem, vmem, vmem],
        out_specs=vmem,
        scratch_shapes=[
            pltpu.VMEM((rows, HD), jnp.bfloat16),
            pltpu.VMEM((5 * GROUP * BLOCK, HD), jnp.bfloat16),
            pltpu.VMEM((5 * GROUP * BLOCK, HD), jnp.bfloat16),
            pltpu.VMEM((5, rows, GROUP * BLOCK), jnp.float32),
            pltpu.VMEM((rows, BLOCK), jnp.float32),
            pltpu.VMEM((rows, BLOCK), jnp.float32),
            pltpu.VMEM((rows, HD), jnp.float32),
        ],
        compiler_params=pltpu.CompilerParams(vmem_limit_bytes=VMEM_LIMIT),
        name="attend",
    )(lists, counts, queries, keys, values, fin)


def table(block_lists, live_counts):
    selected = block_lists.shape[1]
    read = jnp.arange(selected, dtype=jnp.int32)[None, :] < live_counts[:, None]
    flat = jnp.where(read, block_lists, -1).reshape(NZ * NY, 2 * selected)
    owners = jnp.arange(NZ * NY, dtype=jnp.int32)
    hit = (flat >> 3)[:, :, None] == owners[None, None, :]
    return jnp.max(jnp.where(hit, (flat & 7)[:, :, None], 0), axis=1)


def local(
    lin_queries,
    lin_keys,
    lin_values,
    log_decay,
    lin_gate,
    norm_gain,
    soft_queries,
    slab_keys,
    slab_values,
    cache_keys,
    cache_values,
    block_lists,
    live_counts,
):
    blocks = cache_keys.shape[0] // BLOCK
    fin, lin_out = exchange(
        table(block_lists, live_counts),
        cache_keys.reshape(blocks, BLOCK, HD),
        cache_values.reshape(blocks, BLOCK, HD),
        lin_queries,
        lin_keys,
        lin_values,
        lin_gate,
        log_decay,
        norm_gain.reshape(1, -1),
    )
    soft_out = attend(block_lists, live_counts, soft_queries, slab_keys, slab_values, fin)
    return (lin_out, soft_out)


def solution(mesh):
    in_specs = (
        P("ctx", "head"),
        P("ctx", "head"),
        P("ctx", "head"),
        P("ctx", "head"),
        P("ctx", "head"),
        P("head"),
        P("ctx", "head"),
        P("ctx", "head"),
        P("ctx", "head"),
        P("ctx", "head"),
        P("ctx", "head"),
        P(),
        P(),
    )
    out_specs = (P("ctx", "head"), P("ctx", "head"))
    return jax.shard_map(local, mesh=mesh, in_specs=in_specs, out_specs=out_specs, check_vma=False)
```

time: 168 us -> 130 us (0.77)
  the two profiles are of different devices: /device:TPU:16 before, /device:TPU:44 now
where the time goes in v2:
time: 130 us
  Pallas kernels  123 us (95%)
  local copies, waits for them, and re-layouts  4.06 us (3%)
  other arithmetic  2.03 us (2%)
    pallas_call x1, Pallas kernels, exchange(): pl.pallas_call(body, out_shape=(jax.ShapeDtypeStruct((NZ * NY, 2, BLOCK,...  111 us
    pallas_call x1, Pallas kernels, attend(): pl.pallas_call(attend_kernel, out_shape=jax.ShapeDtypeStruct((tok_rows, w...  12.4 us
    unnamed x5, local copies, waits for them, and re-layouts  3.71 us

profile of v2, /device:TPU:44, one launch (start us, length us, event | category | flops | bytes accessed | tf_op | source)
XLA Modules:
  0.0 129.7 jit_solution(13057802322126915857)
XLA Ops:
  0.6 0.7 fusion.2
  1.3 0.1 copy.21
  1.4 0.1 shift_right_arithmetic.15
  1.5 0.1 copy.22
  1.6 0.1 and.15
  1.7 1.3 %select_reduce_fusion.refs_0_ = s32[64,64]{1,0:T(8,128)} fusion(s32[64,32]{1,0:T(8,128)S(1)} %and.15, s32[64,32]{1,0:T(8,128)S(1)} %shift_right_arithmetic.15), kind=kLoop, calls=%fused_computation | loop fusion | flops 389120 | bytes 32768 | tf_op jit(solution)/shard_map/reduce_max | solution.py:605
  3.0 1.4 %copy.24.lists_ref = s32[128,16]{1,0:T(8,128)} copy(s32[128,16]{0,1:T(8,128)} %param.24) | data formatting | bytes 16384 | tf_op args[11]
  4.4 1.5 %copy.23.refs_7_ = f32[256,8]{1,0:T(8,128)} copy(f32[256,8]{0,1:T(8,128)} %param.16) | data formatting | bytes 16384 | tf_op args[3]
  5.9 110.6 %exchange.1 = (bf16[64,2,128,128]{3,2,1,0:T(8,128)(2,1)}, bf16[256,1024]{1,0:T(8,128)(2,1)}) custom-call(s32[64,64]{1,0:T(8,128)} %select_reduce_fusion.refs_0_, bf16[8,128,128]{2,1,0:T(8,128)(2,1)} %bitcast.3, bf16[8,128,128]{2,1,0:T(8,128)(2,1)} %bitcast.4, bf16[256,1024]{1,0:T(8,128)(2,1)} %refs_3_.1, bf16[256,1024]{1,0:T(8,128)(2,1)} %refs_4_.1, ...), custom_call_target="tpu_custom_call" | custom-call | tf_op jit(solution)/shard_map/exchange/pallas_call | solution.py:467
  116.5 0.0 copy-start
  116.5 12.4 %attend.1 = bf16[256,1024]{1,0:T(8,128)(2,1)} custom-call(s32[128,16]{1,0:T(8,128)} %copy.24.lists_ref, s32[128]{0:T(128)} %counts_ref.1, bf16[256,1024]{1,0:T(8,128)(2,1)} %q_ref.1, bf16[256,128]{1,0:T(8,128)(2,1)} %sk_ref.1, bf16[256,128]{1,0:T(8,128)(2,1)} %sv_ref.1, bf16[64,2,128,128]{3,2,1,0:T(8,128)(2,1)} %get-tuple-element.5.fin_ref), custom_call_target="tpu_custom_call" | custom-call | tf_op jit(solution)/shard_map/attend/pallas_call | solution.py:580
  128.9 0.0 copy-done
  128.9 0.8 copy.26
Async XLA Ops:
  116.5 12.4 %copy-start = (bf16[256,1024]{1,0:T(8,128)(2,1)S(1)}, bf16[256,1024]{1,0:T(8,128)(2,1)}, u32[]{:S(2)}) copy-start(bf16[256,1024]{1,0:T(8,128)(2,1)} %get-tuple-element.10) | copy-start | bytes 1572868

commit v3 on v2

--- a/solution.py
+++ b/solution.py
@@ -20,6 +20,8 @@
 NT = (((1,), (1,)), ((), ()))
 TN = (((0,), (0,)), ((), ()))
 LAST = 6
+CHUNKS = 4
+PER = 16 // CHUNKS
 HIGHEST = lax.Precision.HIGHEST
 
 
@@ -75,8 +77,7 @@
 
     barrier = pltpu.get_barrier_semaphore()
     friends = [at(z, yplus(r)) for r in range(1, NY)]
-    friends += [at(zplus(r), y) for r in range(1, NZ)]
-    friends += [at(zplus(k), yplus(r)) for k in (1, 2, NZ - 1, NZ - 2) for r in range(1, NY)]
+    friends += [at(zplus(1), y), at(zplus(NZ - 1), y)]
     friends += [beside(r) for r in range(1, heads)]
     for friend in friends:
         pl.semaphore_signal(barrier, inc=1, device_id=friend, device_id_type=MESH)
@@ -90,12 +91,13 @@
     ring = {}
 
     def send_ring(sign, d, c):
-        half = pl.ds(4 * (c % 2), 4)
-        src = (ck_ref, cv_ref)[c // 2] if d == 1 else bufs[sign, d - 1][c // 2]
+        kind = c * 2 // CHUNKS
+        half = pl.ds(PER * c % 8, PER)
+        src = (ck_ref, cv_ref)[kind] if d == 1 else bufs[sign, d - 1][kind]
         k = 0 if sign > 0 else 1
         made = copy(
             src.at[half],
-            bufs[sign, d][c // 2].at[half],
+            bufs[sign, d][kind].at[half],
             scr["ring_s"].at[k, d - 1, c],
             scr["ring_r"].at[k, d - 1, c],
             at(zplus(1 if sign > 0 else NZ - 1), y),
@@ -103,22 +105,31 @@
         ring[sign, d, c] = made
         made.start()
 
-    for c in range(4):
+    for c in range(CHUNKS):
         send_ring(1, 1, c)
         send_ring(-1, 1, c)
 
+    def spread():
+        for k in range(NZ // 2):
+            for n, to in enumerate((zplus(1), zplus(NZ - 1))):
+                pl.semaphore_signal(
+                    scr["near"].at[n], inc=1, device_id=at(to, y), device_id_type=MESH
+                )
+            for n in range(2):
+                pl.semaphore_wait(scr["near"].at[n], 1)
+
     decay = ld_ref[...]
-    tokens = decay.shape[0]
+    tokens = decay.shape[1]
     row_id = lax.broadcasted_iota(jnp.int32, (tokens, tokens), 0)
     col_id = lax.broadcasted_iota(jnp.int32, (tokens, tokens), 1)
     triangle = jnp.where(col_id <= row_id, 1.0, 0.0).astype(jnp.float32)
     down_all = scr["down"]
     down_all[...] = lax.dot_general(
-        triangle, decay, (((1,), (0,)), ((), ())), precision=HIGHEST, preferred_element_type=jnp.float32
+        triangle, decay, NT, precision=HIGHEST, preferred_element_type=jnp.float32
     )
     across_all = scr["across"]
     across_all[...] = lax.dot_general(
-        decay, triangle, (((0,), (1,)), ((), ())), precision=HIGHEST, preferred_element_type=jnp.float32
+        decay, triangle, NT, precision=HIGHEST, preferred_element_type=jnp.float32
     )
 
     def silu(u):
@@ -147,25 +158,30 @@
     yall, rz, tz, zr, zt = scr["yall"], scr["rz"], scr["tz"], scr["zr"], scr["zt"]
     ez, er, eq, pre, ent = scr["ez"], scr["er"], scr["eq"], scr["pre"], scr["ent"]
 
+    def wanted(source, zz, yy):
+        block = 2 * (zz * NY + yy)
+        return jnp.maximum(sel_ref[source, block], sel_ref[source, block + 1])
+
     stage, far = scr["stage"], scr["far"]
-    picks = []
+    picks, selves = [], []
 
     def pick(n, offset, refs, kinds):
         source = zplus(offset) * NY + y
         for r in range(NY):
-            spot = sel_ref[z * NY + yplus(r), source]
+            spot = wanted(source, z, yplus(r))
             for kind in kinds:
-                block = refs[kind][spot]
-                if r == 0:
-                    fin_ref[source, kind] = block
-                else:
-                    stage[n, r - 1, kind] = block
+                stage[n, r, kind] = refs[kind][spot]
         out = []
-        for r in range(1, NY):
+        for r in range(NY):
             for kind in kinds if len(kinds) == 1 else (None,):
-                a, b, c = stage.at[n, r - 1], fin_ref.at[source], 0
+                a, b, c = stage.at[n, r], fin_ref.at[source], 0
                 if kind is not None:
                     a, b, c = a.at[kind], b.at[kind], kind
+                if r == 0:
+                    made = pltpu.make_async_copy(a, b, scr["self_s"].at[n, c])
+                    made.start()
+                    selves.append(made)
+                    continue
                 out.append(
                     copy(
                         a,
@@ -187,7 +203,7 @@
             for r in range(NY):
                 if beyond == 2 and (r < 2) != (sign > 0):
                     continue
-                spot = sel_ref[to * NY + yplus(r), source]
+                spot = wanted(source, to, yplus(r))
                 far[k, beyond - 1, r, kind] = bufs[sign, LAST][kind][spot]
                 out.append(
                     copy(
@@ -359,7 +375,7 @@
     waiting = pick(0, 0, (own_k, own_v), (0, 1))
     tasks = {
         (1, 2): [row_totals],
-        (1, 3): [send_totals],
+        (1, 3): [spread, send_totals],
         (2, 0): [lambda: intra(0)],
         (2, 1): [lambda: intra(1)],
         (2, 2): [lambda: intra(2)],
@@ -374,7 +390,7 @@
         (5, 2): [send_members],
     }
     for d in range(1, LAST + 1):
-        for c in range(4):
+        for c in range(CHUNKS):
             for sign in (1, -1):
                 ring[sign, d, c].wait_recv()
                 if d < LAST:
@@ -382,10 +398,11 @@
             for made in waiting:
                 made.start()
             waiting = []
-            for task in tasks.get((d, c), []):
+            quarter, rest = divmod((c + 1) * 4, CHUNKS)
+            for task in tasks.get((d, quarter - 1), []) if rest == 0 else []:
                 task()
-            if d == LAST and c % 2 == 1:
-                kind = c // 2
+            if d == LAST and 2 * (c + 1) % CHUNKS == 0:
+                kind = c * 2 // CHUNKS
                 waiting = pick_far(1, kind) + pick_far(-1, kind)
                 waiting += pick(2 * d - 1, NZ - d, bufs[1, d], (kind,))
                 waiting += pick(2 * d, d, bufs[-1, d], (kind,))
@@ -403,6 +420,8 @@
     gate()
     for made in picks:
         made.wait_recv()
+    for made in selves:
+        made.wait()
     for made in sends:
         made.wait_send()
 
@@ -415,7 +434,7 @@
         "bufs": [pltpu.VMEM((8, BLOCK, HD), jnp.bfloat16)] * (4 * LAST),
         "own_k": pltpu.VMEM((8, BLOCK, HD), jnp.bfloat16),
         "own_v": pltpu.VMEM((8, BLOCK, HD), jnp.bfloat16),
-        "stage": pltpu.VMEM((shards, NY - 1, 2, BLOCK, HD), jnp.bfloat16),
+        "stage": pltpu.VMEM((shards, NY, 2, BLOCK, HD), jnp.bfloat16),
         "far": pltpu.VMEM((2, 2, NY, 2, BLOCK, HD), jnp.bfloat16),
         "lq": pltpu.VMEM((tokens, width), jnp.bfloat16),
         "lk": pltpu.VMEM((tokens, width), jnp.bfloat16),
@@ -437,11 +456,13 @@
         "er": pltpu.VMEM((NZ, 16, HD), jnp.bfloat16),
         "eq": pltpu.VMEM((NY, 256, HD), jnp.float32),
         "ent": pltpu.VMEM((NY, 256, HD), jnp.float32),
+        "near": pltpu.SemaphoreType.REGULAR((2,)),
         "in_s": dma((6,)),
-        "ring_s": dma((2, LAST, 4)),
-        "ring_r": dma((2, LAST, 4)),
+        "ring_s": dma((2, LAST, CHUNKS)),
+        "ring_r": dma((2, LAST, CHUNKS)),
         "pick_s": dma((shards, NY - 1, 2)),
         "pick_r": dma((shards, NY - 1, 2)),
+        "self_s": dma((shards, 2)),
         "far_s": dma((2, 2, NY, 2)),
         "far_r": dma((2, 2, NY, 2)),
         "ya_s": dma((NY - 1,)),
@@ -463,7 +484,7 @@
         exchange_kernel(*refs[:11], jax.tree.unflatten(tree, refs[11:]))
 
     vmem = pl.BlockSpec(memory_space=pltpu.VMEM)
-    hbm = pl.BlockSpec(memory_space=pl.ANY)
+    hbm = pl.BlockSpec(memory_space=pltpu.HBM)
     return pl.pallas_call(
         body,
         out_shape=(
@@ -471,7 +492,7 @@
             jax.ShapeDtypeStruct((tokens, width), jnp.bfloat16),
         ),
         in_specs=[pl.BlockSpec(memory_space=pltpu.SMEM)] + [hbm] * 6 + [vmem] * 2,
-        out_specs=(vmem, vmem),
+        out_specs=(hbm, vmem),
         scratch_shapes=flat,
         compiler_params=pltpu.CompilerParams(
             collective_id=0, has_side_effects=True, vmem_limit_bytes=VMEM_LIMIT
@@ -487,7 +508,7 @@
     me = lax.axis_index("ctx")
     factor = math.log2(math.e) / math.sqrt(HD)
     heads = q_ref.shape[1] // HD
-    selected = lists_ref.shape[1]
+    selected = lists_ref.shape[0]
     rows = heads * BLOCK
     chunk = BLOCK
     wide = GROUP * BLOCK
@@ -507,7 +528,7 @@
             keys[BLOCK : 2 * BLOCK] = sk_ref[0:BLOCK]
             values[BLOCK : 2 * BLOCK] = sv_ref[0:BLOCK]
         for j in range(selected):
-            source = lists_ref[query_block, j] >> 3
+            source = lists_ref[j, query_block] >> 3
             place = pl.ds((own + j) * BLOCK, BLOCK)
             keys[place] = fin_ref[source, 0]
             values[place] = fin_ref[source, 1]
@@ -596,13 +617,12 @@
     )(lists, counts, queries, keys, values, fin)
 
 
-def table(block_lists, live_counts):
-    selected = block_lists.shape[1]
-    read = jnp.arange(selected, dtype=jnp.int32)[None, :] < live_counts[:, None]
-    flat = jnp.where(read, block_lists, -1).reshape(NZ * NY, 2 * selected)
+def table(lists, counts):
+    entry = jnp.arange(lists.shape[0], dtype=jnp.int32)[:, None]
+    flat = jnp.where(entry < counts[None, :], lists, -1)
     owners = jnp.arange(NZ * NY, dtype=jnp.int32)
-    hit = (flat >> 3)[:, :, None] == owners[None, None, :]
-    return jnp.max(jnp.where(hit, (flat & 7)[:, :, None], 0), axis=1)
+    hit = (flat >> 3)[:, None, :] == owners[None, :, None]
+    return jnp.max(jnp.where(hit, (flat & 7)[:, None, :], 0), axis=0)
 
 
 def local(
@@ -622,17 +642,17 @@
 ):
     blocks = cache_keys.shape[0] // BLOCK
     fin, lin_out = exchange(
-        table(block_lists, live_counts),
+        table(block_lists.T, live_counts),
         cache_keys.reshape(blocks, BLOCK, HD),
         cache_values.reshape(blocks, BLOCK, HD),
         lin_queries,
         lin_keys,
         lin_values,
         lin_gate,
-        log_decay,
+        log_decay.T,
         norm_gain.reshape(1, -1),
     )
-    soft_out = attend(block_lists, live_counts, soft_queries, slab_keys, slab_values, fin)
+    soft_out = attend(block_lists.T, live_counts, soft_queries, slab_keys, slab_values, fin)
     return (lin_out, soft_out)
 
 

time: 130 us -> 125 us (0.962)
  the two profiles are of different devices: /device:TPU:44 before, /device:TPU:2 now
where the time goes in v3:
time: 125 us; the launch traced here: 124 us
  Pallas kernels  121 us (97%)
  other arithmetic  1.41 us (1%)
    pallas_call x1, Pallas kernels, exchange(): pl.pallas_call(body, out_shape=(jax.ShapeDtypeStruct((NZ * NY, 2, BLOCK,...  110 us
    pallas_call x1, Pallas kernels, attend(): pl.pallas_call(attend_kernel, out_shape=jax.ShapeDtypeStruct((tok_rows, w...  11.4 us

profile of v3, /device:TPU:2, one launch (start us, length us, event | category | flops | bytes accessed | tf_op | source)
XLA Modules:
  0.0 124.0 jit_solution(1256726983044869083)
XLA Ops:
  0.6 0.7 fusion.2
  1.4 0.7 select_reduce_fusion.refs_0_
  2.0 109.7 %exchange.1 = (bf16[64,2,128,128]{3,2,1,0:T(8,128)(2,1)}, bf16[256,1024]{1,0:T(8,128)(2,1)}) custom-call(s32[64,128]{1,0:T(8,128)} %select_reduce_fusion.refs_0_, bf16[8,128,128]{2,1,0:T(8,128)(2,1)} %bitcast.7, bf16[8,128,128]{2,1,0:T(8,128)(2,1)} %bitcast.8, bf16[256,1024]{1,0:T(8,128)(2,1)} %refs_3_.1, bf16[256,1024]{1,0:T(8,128)(2,1)} %refs_4_.1, ...), custom_call_target="tpu_custom_call" | custom-call | tf_op jit(solution)/shard_map/exchange/pallas_call | solution.py:488
  111.8 0.0 copy-start
  111.8 11.4 %attend.1 = bf16[256,1024]{1,0:T(8,128)(2,1)} custom-call(s32[16,128]{1,0:T(8,128)} %bitcast.9, s32[128]{0:T(128)} %counts_ref.1, bf16[256,1024]{1,0:T(8,128)(2,1)} %q_ref.1, bf16[256,128]{1,0:T(8,128)(2,1)} %sk_ref.1, bf16[256,128]{1,0:T(8,128)(2,1)} %sv_ref.1, bf16[64,2,128,128]{3,2,1,0:T(8,128)(2,1)} %get-tuple-element.5.fin_ref), custom_call_target="tpu_custom_call" | custom-call | tf_op jit(solution)/shard_map/attend/pallas_call | solution.py:601
  123.2 0.0 copy-done
  123.2 0.8 copy.16
Async XLA Ops:
  111.8 11.4 %copy-start = (bf16[256,1024]{1,0:T(8,128)(2,1)S(1)}, bf16[256,1024]{1,0:T(8,128)(2,1)}, u32[]{:S(2)}) copy-start(bf16[256,1024]{1,0:T(8,128)(2,1)} %get-tuple-element.10) | copy-start | bytes 1572868
